TPU v7x, 32 devices: a whole 2x2x4 slice. The times are simulated.
32 devices in a mesh: dom: 8 (over z, core), grp: 4 (over y, x).
Axes of the slice: x: 2, y: 2, z: 4, core: 2. Of those that a mesh axis runs over, the one named last changes fastest.
Arguments:
- feats: bfloat16 [8192, 256], P(('dom', 'grp')), may hold values from -6 to 6
- w_self: bfloat16 [256, 256], replicated, may hold values from -0.375 to 0.375
- w_neigh: bfloat16 [256, 256], replicated, may hold values from -0.375 to 0.375
- local_tiles: bfloat16 [64, 3, 128, 128], P(('dom', 'grp')), may hold values from -0.15625 to 0.15625
- local_cols: int32 [64, 3], P(('dom', 'grp')), may hold values from 0 to 7, as said below
- cut_tiles: bfloat16 [64, 10, 128, 128], P(('dom', 'grp')), may hold values from -0.15625 to 0.15625
- cut_src: int32 [64, 10], P(('dom', 'grp')), may hold values from 0 to 7, as said below
- send_block: int32 [32, 8], P(('dom', 'grp')), may hold values from 0 to 1
- send_live: int32 [32, 8], P(('dom', 'grp')), may hold values from 0 to 1, as said below
- cotangent: bfloat16 [8192, 256], P(('dom', 'grp')), may hold values from -0.0625 to 0.0625
Outputs:
- layer_out: bfloat16 [8192, 256], P(('dom', 'grp'))
- grad_self: float32 [256, 256], replicated
- grad_neigh: float32 [256, 256], replicated
Inputs may be any that keep to these rules, and one draw needn't show every extreme that they name: `local_cols`: the 3 column blocks of one row block are distinct. `cut_src`: 0 marks an empty slot; the share of filled slots differs from partition to partition. send_live[e, p] is 1 exactly when some row block of device p * 4 + g (g the position of e) has a cut slot with offset naming e's partition; it is 0 where p is e's own partition.
All inputs are finite; a program needn't handle non-finite values.
Results may differ from a plain program's by a relative error of at most 0.0056.
Values may be sent and summed in bfloat16 or wider, within the bound.
A program may use at most 64 MiB of HBM per device.

v0:
```python
import jax
import jax.numpy as jnp
from jax import lax
from jax.sharding import PartitionSpec as P


def body(
    feats,
    w_self,
    w_neigh,
    local_tiles,
    local_cols,
    cut_tiles,
    cut_src,
    send_block,
    send_live,
    cotangent,
):
    row_blocks = local_tiles.shape[0]
    block_size = local_tiles.shape[2]
    features = feats.shape[1]
    partitions = lax.axis_size("dom")
    own_blocks = feats.reshape(row_blocks, block_size, features)
    gathered = lax.all_gather(feats, "grp", axis=0, tiled=True)
    picked = gathered.reshape(-1, block_size, features)[local_cols]
    aggregate_sum = jnp.einsum(
        "rkij,rkjf->rif", local_tiles, picked, preferred_element_type=jnp.float32
    )
    outgoing = own_blocks[send_block[0]] * send_live[0][:, None, None].astype(jnp.bfloat16)
    received = lax.all_to_all(outgoing, "dom", split_axis=0, concat_axis=0, tiled=True)
    source = (lax.axis_index("dom") + cut_src) % partitions
    remote = received[source]
    aggregate_sum = aggregate_sum + jnp.einsum(
        "rkij,rkjf->rif", cut_tiles, remote, preferred_element_type=jnp.float32
    )
    agg = aggregate_sum.reshape(row_blocks * block_size, features).astype(jnp.bfloat16)
    preact = jnp.dot(feats, w_self, preferred_element_type=jnp.float32) + jnp.dot(
        agg, w_neigh, preferred_element_type=jnp.float32
    )
    sigmoid = jax.nn.sigmoid(preact)
    layer_out = (preact * sigmoid).astype(jnp.bfloat16)
    grad_pre = (cotangent.astype(jnp.float32) * sigmoid * (1.0 + preact * (1.0 - sigmoid))).astype(
        jnp.bfloat16
    )
    grad_own = jnp.dot(feats.T, grad_pre, preferred_element_type=jnp.float32)
    grad_agg = jnp.dot(agg.T, grad_pre, preferred_element_type=jnp.float32)
    stacked = jnp.concatenate([grad_own, grad_agg], axis=0)
    shared = lax.psum_scatter(stacked, "grp", scatter_dimension=0, tiled=True)
    shared = lax.psum(shared, "dom")
    summed = lax.all_gather(shared, "grp", axis=0, tiled=True)
    return (layer_out, summed[:features], summed[features:])


def solution(mesh):
    return jax.shard_map(
        body,
        mesh=mesh,
        in_specs=(
            P(("dom", "grp"), None),
            P(),
            P(),
            P(("dom", "grp"), None, None, None),
            P(("dom", "grp"), None),
            P(("dom", "grp"), None, None, None),
            P(("dom", "grp"), None),
            P(("dom", "grp"), None),
            P(("dom", "grp"), None),
            P(("dom", "grp"), None),
        ),
        out_specs=(P(("dom", "grp"), None), P(), P()),
        check_vma=False,
    )
```

profile of v0, /device:TPU:0, one launch (start us, length us, event | category | flops | bytes accessed | tf_op | source)
XLA Modules:
  0.0 135.9 jit_solution(555693463951138174)
XLA Ops:
  7.2 0.0 copy-start
  7.2 0.7 fusion.3
  7.9 0.7 convert_bitcast_fusion
  8.6 1.5 %gather_fusion.1 = bf16[8,128,256]{2,1,0:T(8,128)(2,1)S(1)} fusion(bf16[2,128,256]{2,1,0:T(8,128)(2,1)} %bitcast.37, s32[1024]{0:T(1024)S(1)} %pad_clamp_fusion.1), kind=kCustom, calls=%fused_computation.1 | custom fusion | bytes 1048608 | tf_op jit(solution)/shard_map/gather | solution.py:29
  10.1 0.0 copy-start.4
  10.1 0.0 copy-start.5
  10.1 0.0 copy-start.1
  10.1 0.9 broadcast_multiply_fusion
  11.0 0.0 copy-start.2
  11.0 6.5 %all-to-all-start = ((bf16[8,128,256]{2,1,0:T(8,128)(2,1)}), bf16[8,128,256]{2,1,0:T(8,128)(2,1)S(1)}, u32[]{:S(2)}, u32[]{:S(2)}) async-start(bf16[8,128,256]{2,1,0:T(8,128)(2,1)} %broadcast_multiply_fusion), calls=%async_computation | async-start | bytes 1048576 | tf_op jit(solution)/shard_map/all_to_all | solution.py:30
  17.5 0.0 copy-start.3
  17.5 0.0 reduce-scatter.2.cloned.1.call-start
  17.5 0.0 copy-done.4
  17.6 0.1 reshape.70
  17.6 0.0 copy-done.5
  17.6 0.1 reshape.54
  17.7 0.0 copy-done.1
  17.7 10.6 %all_gather.6 = bf16[1024,256]{1,0:T(8,128)(2,1)S(1)} all-gather(bf16[256,256]{1,0:T(8,128)(2,1)S(1)} %copy-done.1), channel_id=1, replica_groups=mesh['dom'=8,'grp'=4] {'grp'}, dimensions={0}, use_global_device_ids=true | all-gather | bytes 655360 | tf_op jit(solution)/shard_map/all_gather | solution.py:24
  28.3 0.6 gather_fusion
  28.9 0.0 copy-done.2
  28.9 0.2 convolution_bitcast_fusion
  29.2 0.0 copy-done.3
  29.2 0.2 fusion.5
  29.4 3.5 %all-to-all-done = bf16[8,128,256]{2,1,0:T(8,128)(2,1)S(1)} async-done(((bf16[8,128,256]{2,1,0:T(8,128)(2,1)}), bf16[8,128,256]{2,1,0:T(8,128)(2,1)S(1)}, u32[]{:S(2)}, u32[]{:S(2)}) %all-to-all-start) | async-done | bytes 524320 | tf_op jit(solution)/shard_map/all_to_all | solution.py:30
  32.8 0.6 gather_fusion.2
  33.5 0.0 copy-start.6
  33.5 0.0 copy-start.7
  33.5 0.0 copy-done
  33.5 0.3 fusion.1
  33.9 0.5 copy-done.6
  34.4 0.1 copy-done.7
  34.4 0.9 multiply_convert_fusion
  35.4 0.2 fusion.6
  35.6 0.2 convolution_bitcast_fusion.1
  35.8 0.8 pad_maximum_fusion
  36.7 0.0 reduce-scatter.2.cloned.1.call-update
  36.7 0.0 all-reduce.2.cloned.1.call-start
  36.8 23.8 %reduce-scatter.2.cloned.1.call-done = f32[128,256]{1,0:T(8,128)} async-done(((f32[512,256]{1,0:T(8,128)}), f32[128,256]{1,0:T(8,128)}) %reduce-scatter.2.cloned.1.call-update) | async-done | bytes 131088 | tf_op jit(solution)/shard_map/reduce_scatter | solution.py:48
  60.5 0.0 all-reduce.2.cloned.1.call-update
  60.6 56.7 %all-reduce.2.cloned.1.call-done = f32[128,256]{1,0:T(8,128)} async-done(((f32[128,256]{1,0:T(8,128)}), f32[128,256]{1,0:T(8,128)}) %all-reduce.2.cloned.1.call-update) | async-done | bytes 131088 | tf_op jit(solution)/shard_map/psum | solution.py:49
  117.2 11.0 %all_gather.7 = f32[512,256]{1,0:T(8,128)S(1)} all-gather(f32[128,256]{1,0:T(8,128)} %all-reduce.2.cloned.1.call-done), channel_id=1, replica_groups=mesh['dom'=8,'grp'=4] {'grp'}, dimensions={0}, use_global_device_ids=true | all-gather | bytes 655360 | tf_op jit(solution)/shard_map/all_gather | solution.py:50
  128.3 0.8 fusion.4
  (5 shorter events, 0.0 us)
Async XLA Ops:
  7.2 26.3 %copy-start = (bf16[2,10,128,128]{3,2,1,0:T(8,128)(2,1)S(1)}, bf16[2,10,128,128]{3,2,1,0:T(8,128)(2,1)}, u32[]{:S(2)}) copy-start(bf16[2,10,128,128]{3,2,1,0:T(8,128)(2,1)} %param.15) | copy-start | bytes 1966084
  10.1 7.5 %copy-start.4 = (s32[2,10]{1,0:T(2,128)S(1)}, s32[2,10]{1,0:T(2,128)}, u32[]{:S(2)}) copy-start(s32[2,10]{1,0:T(2,128)} %param.16) | copy-start | bytes 244
  10.1 7.6 %copy-start.5 = (s32[2,3]{1,0:T(2,128)S(1)}, s32[2,3]{1,0:T(2,128)}, u32[]{:S(2)}) copy-start(s32[2,3]{1,0:T(2,128)} %param.14) | copy-start | bytes 76
  10.1 7.6 %copy-start.1 = (bf16[256,256]{1,0:T(8,128)(2,1)S(1)}, bf16[256,256]{1,0:T(8,128)(2,1)}, u32[]{:S(2)}) copy-start(bf16[256,256]{1,0:T(8,128)(2,1)} %param.10) | copy-start | bytes 393220
  11.0 17.9 %copy-start.2 = (bf16[2,3,128,128]{3,2,1,0:T(8,128)(2,1)S(1)}, bf16[2,3,128,128]{3,2,1,0:T(8,128)(2,1)}, u32[]{:S(2)}) copy-start(bf16[2,3,128,128]{3,2,1,0:T(8,128)(2,1)} %param.13) | copy-start | bytes 589828
  11.0 21.8 %all-to-all-start = ((bf16[8,128,256]{2,1,0:T(8,128)(2,1)}), bf16[8,128,256]{2,1,0:T(8,128)(2,1)S(1)}, u32[]{:S(2)}, u32[]{:S(2)}) async-start(bf16[8,128,256]{2,1,0:T(8,128)(2,1)} %broadcast_multiply_fusion), calls=%async_computation | async-start | bytes 1048576 | tf_op jit(solution)/shard_map/all_to_all | solution.py:30
  17.5 11.7 %copy-start.3 = (bf16[256,256]{1,0:T(8,128)(2,1)S(1)}, bf16[256,256]{1,0:T(8,128)(2,1)}, u32[]{:S(2)}) copy-start(bf16[256,256]{1,0:T(8,128)(2,1)} %param.11) | copy-start | bytes 393220
  17.5 43.1 %reduce-scatter.2.cloned.1.call-start = ((), (), s32[]{:S(2)}) async-start(), calls=%async_computation.2 | async-start | bytes 655360 | tf_op jit(solution)/shard_map/reduce_scatter | solution.py:48
  33.5 0.9 copy-start.6
  33.5 1.0 copy-start.7
  36.7 80.5 %all-reduce.2.cloned.1.call-start = ((), (), s32[]{:S(2)}) async-start(), calls=%async_computation.3 | async-start | bytes 262144 | tf_op jit(solution)/shard_map/psum | solution.py:49
Sparse Core Ops, SparseCore 0:
  36.8 23.6 reduce-scatter.1
  63.0 54.2 all-reduce.1
where the time goes:
time: 136 us
  waiting for transfers between devices  84 us (62%)
  blocking collectives  21.6 us (16%)
  between operations  14.2 us (10%)
  starting transfers between devices  6.54 us (5%)
  local copies, waits for them, and re-layouts  4.3 us (3%)
  other arithmetic  3.17 us (2%)
  matrix products  2.14 us (2%)
    psum x1, waiting for transfers between devices, body(): shared = lax.psum(shared, 'dom')  56.7 us
    reduce_scatter x1, waiting for transfers between devices, body(): shared = lax.psum_scatter(stacked, 'grp', scatter_dimension=0, tiled=True)  23.8 us
    all_gather x1, blocking collectives, body(): summed = lax.all_gather(shared, 'grp', axis=0, tiled=True)  11 us
    all_gather x1, blocking collectives, body(): gathered = lax.all_gather(feats, 'grp', axis=0, tiled=True)  10.6 us
    all_to_all x1, starting transfers between devices, body(): lax.all_to_all(outgoing, 'dom', split_axis=0, concat_axis=0, tiled=True)  6.46 us
    all_to_all x1, waiting for transfers between devices, body(): lax.all_to_all(outgoing, 'dom', split_axis=0, concat_axis=0, tiled=True)  3.46 us
  transfers between devices with their start and end apart: 3, of which 3 were waited for; matrix products, arithmetic and copies ran while one was open for 1% of the time, Pallas kernels for 0%

commit v1 on v0

--- a/solution.py
+++ b/solution.py
@@ -46,7 +46,8 @@
     grad_agg = jnp.dot(agg.T, grad_pre, preferred_element_type=jnp.float32)
     stacked = jnp.concatenate([grad_own, grad_agg], axis=0)
     shared = lax.psum_scatter(stacked, "grp", scatter_dimension=0, tiled=True)
-    shared = lax.psum(shared, "dom")
+    parts = lax.all_gather(shared, "dom", axis=0, tiled=False)
+    shared = parts.sum(axis=0)
     summed = lax.all_gather(shared, "grp", axis=0, tiled=True)
     return (layer_out, summed[:features], summed[features:])
 

time: 136 us -> 104 us (0.76)
  waiting for transfers between devices: 84 us -> 51.1 us
    psum x1 -> x0, waiting for transfers between devices: 56.7 us -> none  [body(): shared = lax.psum(shared, 'dom')]
    all_gather x0 -> x1, waiting for transfers between devices: none -> 23.8 us  [body(): parts = lax.all_gather(shared, 'dom', axis=0, tiled=False)]
where the time goes in v1:
time: 104 us; the launch traced here: 103 us
  waiting for transfers between devices  51.1 us (49%)
  blocking collectives  20.6 us (20%)
  between operations  14.2 us (14%)
  starting transfers between devices  6.54 us (6%)
  other arithmetic  4.47 us (4%)
  local copies, waits for them, and re-layouts  4.3 us (4%)
  matrix products  2.14 us (2%)
    reduce_scatter x1, waiting for transfers between devices, body(): shared = lax.psum_scatter(stacked, 'grp', scatter_dimension=0, tiled=True)  23.8 us
    all_gather x1, waiting for transfers between devices, body(): parts = lax.all_gather(shared, 'dom', axis=0, tiled=False)  23.8 us
    all_gather x1, blocking collectives, body(): gathered = lax.all_gather(feats, 'grp', axis=0, tiled=True)  10.6 us
    all_gather x1, blocking collectives, body(): summed = lax.all_gather(shared, 'grp', axis=0, tiled=True)  9.99 us
    all_to_all x1, starting transfers between devices, body(): lax.all_to_all(outgoing, 'dom', split_axis=0, concat_axis=0, tiled=True)  6.46 us
    all_to_all x1, waiting for transfers between devices, body(): lax.all_to_all(outgoing, 'dom', split_axis=0, concat_axis=0, tiled=True)  3.46 us
  transfers between devices with their start and end apart: 3, of which 3 were waited for; matrix products, arithmetic and copies ran while one was open for 1% of the time, Pallas kernels for 0%

profile of v1, /device:TPU:0, one launch (start us, length us, event | category | flops | bytes accessed | tf_op | source)
XLA Modules:
  0.0 103.3 jit_solution(526052333743112662)
XLA Ops:
  7.2 0.0 copy-start
  7.2 0.7 fusion.3
  7.9 0.7 convert_bitcast_fusion
  8.6 1.5 %gather_fusion.1 = bf16[8,128,256]{2,1,0:T(8,128)(2,1)S(1)} fusion(bf16[2,128,256]{2,1,0:T(8,128)(2,1)} %bitcast.38, s32[1024]{0:T(1024)S(1)} %pad_clamp_fusion.1), kind=kCustom, calls=%fused_computation.1 | custom fusion | bytes 1048608 | tf_op jit(solution)/shard_map/gather | solution.py:29
  10.1 0.0 copy-start.4
  10.1 0.0 copy-start.5
  10.1 0.0 copy-start.1
  10.1 0.9 broadcast_multiply_fusion
  11.0 0.0 copy-start.2
  11.0 6.5 %all-to-all-start = ((bf16[8,128,256]{2,1,0:T(8,128)(2,1)}), bf16[8,128,256]{2,1,0:T(8,128)(2,1)S(1)}, u32[]{:S(2)}, u32[]{:S(2)}) async-start(bf16[8,128,256]{2,1,0:T(8,128)(2,1)} %broadcast_multiply_fusion), calls=%async_computation | async-start | bytes 1048576 | tf_op jit(solution)/shard_map/all_to_all | solution.py:30
  17.5 0.0 copy-start.3
  17.5 0.0 reduce-scatter.2.cloned.1.call-start
  17.5 0.0 copy-done.4
  17.6 0.1 reshape.70
  17.6 0.0 copy-done.5
  17.6 0.1 reshape.54
  17.7 0.0 copy-done.1
  17.7 10.6 %all_gather.12 = bf16[1024,256]{1,0:T(8,128)(2,1)S(1)} all-gather(bf16[256,256]{1,0:T(8,128)(2,1)S(1)} %copy-done.1), channel_id=1, replica_groups=mesh['dom'=8,'grp'=4] {'grp'}, dimensions={0}, use_global_device_ids=true | all-gather | bytes 655360 | tf_op jit(solution)/shard_map/all_gather | solution.py:24
  28.3 0.6 gather_fusion
  28.9 0.0 copy-done.2
  28.9 0.2 convolution_bitcast_fusion
  29.2 0.0 copy-done.3
  29.2 0.2 fusion.5
  29.4 3.5 %all-to-all-done = bf16[8,128,256]{2,1,0:T(8,128)(2,1)S(1)} async-done(((bf16[8,128,256]{2,1,0:T(8,128)(2,1)}), bf16[8,128,256]{2,1,0:T(8,128)(2,1)S(1)}, u32[]{:S(2)}, u32[]{:S(2)}) %all-to-all-start) | async-done | bytes 524320 | tf_op jit(solution)/shard_map/all_to_all | solution.py:30
  32.8 0.6 gather_fusion.2
  33.5 0.0 copy-start.6
  33.5 0.0 copy-start.7
  33.5 0.0 copy-done
  33.5 0.3 fusion.1
  33.9 0.5 copy-done.6
  34.4 0.1 copy-done.7
  34.4 0.9 multiply_convert_fusion
  35.4 0.2 fusion.6
  35.6 0.2 convolution_bitcast_fusion.1
  35.8 0.8 pad_maximum_fusion
  36.7 0.0 reduce-scatter.2.cloned.1.call-update
  36.7 0.0 all-gather.3.cloned.1.call-start
  36.8 23.8 %reduce-scatter.2.cloned.1.call-done = f32[128,256]{1,0:T(8,128)} async-done(((f32[512,256]{1,0:T(8,128)}), f32[128,256]{1,0:T(8,128)}) %reduce-scatter.2.cloned.1.call-update) | async-done | bytes 131088 | tf_op jit(solution)/shard_map/reduce_scatter | solution.py:48
  60.6 0.0 all-gather.3.cloned.1.call-update
  60.6 23.8 %all-gather.3.cloned.1.call-done = f32[1024,256]{1,0:T(8,128)} async-done(((f32[128,256]{1,0:T(8,128)}), f32[1024,256]{1,0:T(8,128)}) %all-gather.3.cloned.1.call-update) | async-done | bytes 1048592 | tf_op jit(solution)/shard_map/all_gather | solution.py:49
  84.4 1.3 %reduce_sum.9 = f32[128,256]{1,0:T(8,128)S(1)} reduce(f32[8,128,256]{2,1,0:T(8,128)} %bitcast.42, f32[]{:T(128)} %constant.31.clone.1), dimensions={0}, to_apply=%region_1.2 | reduce | flops 229376 | bytes 1179652 | tf_op jit(solution)/shard_map/reduce_sum | solution.py:50
  85.7 10.0 %all_gather.15 = f32[512,256]{1,0:T(8,128)S(1)} all-gather(f32[128,256]{1,0:T(8,128)S(1)} %reduce_sum.9), channel_id=1, replica_groups=mesh['dom'=8,'grp'=4] {'grp'}, dimensions={0}, use_global_device_ids=true | all-gather | bytes 655360 | tf_op jit(solution)/shard_map/all_gather | solution.py:51
  95.7 0.8 fusion.4
  (5 shorter events, 0.0 us)
Async XLA Ops:
  7.2 26.3 %copy-start = (bf16[2,10,128,128]{3,2,1,0:T(8,128)(2,1)S(1)}, bf16[2,10,128,128]{3,2,1,0:T(8,128)(2,1)}, u32[]{:S(2)}) copy-start(bf16[2,10,128,128]{3,2,1,0:T(8,128)(2,1)} %param.15) | copy-start | bytes 1966084
  10.1 7.5 %copy-start.4 = (s32[2,10]{1,0:T(2,128)S(1)}, s32[2,10]{1,0:T(2,128)}, u32[]{:S(2)}) copy-start(s32[2,10]{1,0:T(2,128)} %param.16) | copy-start | bytes 244
  10.1 7.6 %copy-start.5 = (s32[2,3]{1,0:T(2,128)S(1)}, s32[2,3]{1,0:T(2,128)}, u32[]{:S(2)}) copy-start(s32[2,3]{1,0:T(2,128)} %param.14) | copy-start | bytes 76
  10.1 7.6 %copy-start.1 = (bf16[256,256]{1,0:T(8,128)(2,1)S(1)}, bf16[256,256]{1,0:T(8,128)(2,1)}, u32[]{:S(2)}) copy-start(bf16[256,256]{1,0:T(8,128)(2,1)} %param.10) | copy-start | bytes 393220
  11.0 17.9 %copy-start.2 = (bf16[2,3,128,128]{3,2,1,0:T(8,128)(2,1)S(1)}, bf16[2,3,128,128]{3,2,1,0:T(8,128)(2,1)}, u32[]{:S(2)}) copy-start(bf16[2,3,128,128]{3,2,1,0:T(8,128)(2,1)} %param.13) | copy-start | bytes 589828
  11.0 21.8 %all-to-all-start = ((bf16[8,128,256]{2,1,0:T(8,128)(2,1)}), bf16[8,128,256]{2,1,0:T(8,128)(2,1)S(1)}, u32[]{:S(2)}, u32[]{:S(2)}) async-start(bf16[8,128,256]{2,1,0:T(8,128)(2,1)} %broadcast_multiply_fusion), calls=%async_computation | async-start | bytes 1048576 | tf_op jit(solution)/shard_map/all_to_all | solution.py:30
  17.5 11.7 %copy-start.3 = (bf16[256,256]{1,0:T(8,128)(2,1)S(1)}, bf16[256,256]{1,0:T(8,128)(2,1)}, u32[]{:S(2)}) copy-start(bf16[256,256]{1,0:T(8,128)(2,1)} %param.11) | copy-start | bytes 393220
  17.5 43.1 %reduce-scatter.2.cloned.1.call-start = ((), (), s32[]{:S(2)}) async-start(), calls=%async_computation.2 | async-start | bytes 655360 | tf_op jit(solution)/shard_map/reduce_scatter | solution.py:48
  33.5 0.9 copy-start.6
  33.5 1.0 copy-start.7
  36.7 47.7 %all-gather.3.cloned.1.call-start = ((), (), s32[]{:S(2)}) async-start(), calls=%async_computation.3 | async-start | bytes 1179648 | tf_op jit(solution)/shard_map/all_gather | solution.py:49
Sparse Core Ops, SparseCore 0:
  36.8 23.7 reduce-scatter.1
  62.3 22.0 all-gather.2
